TPU v7x, 256 devices: a whole 4x4x8 slice. The times are simulated.
256 devices in a mesh: frame: 16 (over x_hi, z), head: 8 (over y, core), dp: 2 (over x_lo).
Axes of the slice: x: 4 (x_hi: 2, x_lo: 2; x = x_hi * 2 + x_lo), y: 4, z: 8, core: 2. Of those that a mesh axis runs over, the one named last changes fastest.
Arguments:
- clip: bfloat16 [2, 4096, 256], P('dp', 'frame'), may hold values from -40 to 40
- block_ids: int32 [2, 4096], P('dp'), may hold values from 0 to 63, never falling along the last dimension, each value on 1 to 128 neighbouring positions
- w_spatial: bfloat16 [9, 256, 256], replicated, may hold values from -0.125 to 0.125
- w_temporal: bfloat16 [3, 256, 256], replicated, may hold values from -0.21875 to 0.21875
- w_query: bfloat16 [256, 2048], P(None, 'head'), may hold values from -0.375 to 0.375
- w_key: bfloat16 [256, 2048], P(None, 'head'), may hold values from -0.375 to 0.375
- w_value: bfloat16 [256, 2048], P(None, 'head'), may hold values from -0.375 to 0.375
- w_out: bfloat16 [2048, 256], P('head'), may hold values from -0.125 to 0.125
- cotangent: bfloat16 [2, 4096, 256], P('dp', 'frame'), may hold values from -6 to 6
Outputs:
- grad_spatial: float32 [9, 256, 256], replicated
- grad_temporal: float32 [3, 256, 256], replicated
- grad_query: float32 [256, 2048], P(None, 'head')
- grad_key: float32 [256, 2048], P(None, 'head')
- grad_value: float32 [256, 2048], P(None, 'head')
- grad_out: float32 [2048, 256], P('head')
Inputs may be any that keep to these rules, and one draw needn't show every extreme that they name: `block_ids`: block numbers never fall along a clip's tokens; every block has 1 to (128) tokens.
All inputs are finite; a program needn't handle non-finite values.
Results may differ from a plain program's by a relative error of at most 0.04.
Values may be sent and summed in bfloat16 or wider, within the bound.
No kernel may reach another device: no remote copies, remote signals or barrier semaphores. Data moves between devices by JAX's collectives and lax.ppermute only.
A program may use at most 128 MiB of HBM per device.

v0:
```python
import jax
import jax.numpy as jnp
from jax import lax
from jax.sharding import PartitionSpec as P

HD = 128
SIDE = 8
NEG_FILL = -1e30


def with_halo(cells, sides, width):
    for axis, dim in sides:
        count = lax.axis_size(axis)
        ends = count - 1
        head = lax.slice_in_dim(cells, 0, width, axis=dim)
        tail = lax.slice_in_dim(cells, cells.shape[dim] - width, cells.shape[dim], axis=dim)
        cells = jnp.concatenate(
            [
                lax.ppermute(tail, axis, [(i, (i + 1) % count) for i in range(ends)]),
                cells,
                lax.ppermute(head, axis, [((i + 1) % count, i) for i in range(ends)]),
            ],
            axis=dim,
        )
    return cells


def spatial_taps(frame_grid, side):
    padded = jnp.pad(frame_grid, ((0, 0), (1, 1), (1, 1), (0, 0)))
    count = frame_grid.shape[0] * side * side
    width = frame_grid.shape[3]
    return [
        padded[:, row_off : row_off + side, col_off : col_off + side, :].reshape(count, width)
        for row_off in range(3)
        for col_off in range(3)
    ]


def silu_slope(pre_act):
    sigma = jax.nn.sigmoid(pre_act)
    return sigma * (1.0 + pre_act * (1.0 - sigma))


def frame_rims(field):
    return with_halo(field, (("frame", 0),), SIDE * SIDE)


def take_head(matrix, which_head):
    return matrix[:, which_head * HD : (which_head + 1) * HD]


def contract_rows(left, right):
    return lax.dot_general(
        left, right, (((0,), (0,)), ((), ())), preferred_element_type=jnp.float32
    )


def on_device(clip, block_ids, w_spatial, w_temporal, w_query, w_key, w_value, w_out, cotangent):
    frames_in = clip[0]
    upstream = cotangent[0]
    clip_blocks = block_ids[0]
    tok_local, channels = frames_in.shape
    frame_len = SIDE * SIDE
    scale = HD ** (-0.5)
    grid = frames_in.reshape(tok_local // frame_len, SIDE, SIDE, channels)
    taps = spatial_taps(grid, SIDE)
    pre_act = jnp.zeros((tok_local, channels), jnp.float32)
    for offset in range(9):
        pre_act = pre_act + jnp.dot(
            taps[offset], w_spatial[offset], preferred_element_type=jnp.float32
        )
    hidden = jax.nn.silu(pre_act).astype(jnp.bfloat16)
    hidden_rim = frame_rims(hidden)
    temporal = jnp.zeros((tok_local, channels), jnp.float32)
    for offset in range(3):
        temporal = temporal + jnp.dot(
            hidden_rim[offset * frame_len : offset * frame_len + tok_local],
            w_temporal[offset],
            preferred_element_type=jnp.float32,
        )
    features = temporal.astype(jnp.bfloat16)
    queries_local = jnp.dot(features, w_query, preferred_element_type=jnp.float32).astype(
        jnp.bfloat16
    )
    keys_local = jnp.dot(features, w_key, preferred_element_type=jnp.float32).astype(jnp.bfloat16)
    values_local = jnp.dot(features, w_value, preferred_element_type=jnp.float32).astype(
        jnp.bfloat16
    )
    keys_every, values_every = (
        lax.all_gather(keys_local, "frame", axis=0, tiled=True),
        lax.all_gather(values_local, "frame", axis=0, tiled=True),
    )
    first_row = lax.axis_index("frame") * tok_local
    grad_attended = jnp.dot(upstream, w_out.T, preferred_element_type=jnp.float32).astype(
        jnp.bfloat16
    )
    queries_held, grad_held = (queries_local, grad_attended)
    held_blocks = lax.dynamic_slice_in_dim(clip_blocks, first_row, tok_local)
    visible = clip_blocks[None, :] <= held_blocks[:, None]
    heads_here = queries_local.shape[1] // HD
    width_here = queries_local.shape[1]
    attended_parts, grad_query_parts, prob_list, score_grads, norm_list, delta_list = (
        [],
        [],
        [],
        [],
        [],
        [],
    )
    for which_head in range(heads_here):
        query_head = take_head(queries_held, which_head)
        key_head = take_head(keys_every, which_head)
        value_head = take_head(values_every, which_head)
        grad_head = take_head(grad_held, which_head)
        scores = jnp.dot(query_head, key_head.T, preferred_element_type=jnp.float32) * scale
        masked = jnp.where(visible, scores, NEG_FILL)
        top = jnp.max(masked, axis=1, keepdims=True)
        total = jnp.sum(jnp.where(visible, jnp.exp(masked - top), 0.0), axis=1, keepdims=True)
        log_norm = top + jnp.log(total)
        probs = jnp.where(visible, jnp.exp(masked - log_norm), 0.0)
        probs_low = probs.astype(jnp.bfloat16)
        attended = jnp.dot(probs_low, value_head, preferred_element_type=jnp.float32).astype(
            jnp.bfloat16
        )
        delta = jnp.sum(
            grad_head.astype(jnp.float32) * attended.astype(jnp.float32), axis=1, keepdims=True
        )
        grad_probs = jnp.dot(grad_head, value_head.T, preferred_element_type=jnp.float32)
        grad_scores = (probs * (grad_probs - delta) * scale).astype(jnp.bfloat16)
        grad_query_parts.append(
            jnp.dot(grad_scores, key_head, preferred_element_type=jnp.float32).astype(jnp.bfloat16)
        )
        attended_parts.append(attended)
        prob_list.append(probs_low)
        score_grads.append(grad_scores)
        norm_list.append(log_norm)
        delta_list.append(delta)
    attended_all = jnp.concatenate(attended_parts, axis=1)
    grad_queries = jnp.concatenate(grad_query_parts, axis=1)
    key_parts = []
    value_parts = []
    for which_head in range(heads_here):
        score_cols = score_grads[which_head]
        prob_cols = prob_list[which_head]
        key_parts.append(contract_rows(score_cols, take_head(queries_held, which_head)))
        value_parts.append(contract_rows(prob_cols, take_head(grad_held, which_head)))
    summed = lax.psum_scatter(
        jnp.concatenate(key_parts + value_parts, axis=1), "frame", scatter_dimension=0, tiled=True
    )
    grad_keys = summed[:, :width_here].astype(jnp.bfloat16)
    grad_values = summed[:, width_here:].astype(jnp.bfloat16)
    grad_wq_local = contract_rows(features, grad_queries)
    grad_wk_local = contract_rows(features, grad_keys)
    grad_wv_local = contract_rows(features, grad_values)
    grad_wo_local = contract_rows(attended_all, upstream)
    back_part = jnp.dot(grad_queries, w_query.T, preferred_element_type=jnp.float32)
    back_part = back_part + jnp.dot(grad_keys, w_key.T, preferred_element_type=jnp.float32)
    back_part = back_part + jnp.dot(grad_values, w_value.T, preferred_element_type=jnp.float32)
    head_sum = lax.psum(back_part, "head")
    grad_features = (head_sum + upstream.astype(jnp.float32)).astype(jnp.bfloat16)
    grad_rim = frame_rims(grad_features)
    grad_wt = jnp.stack(
        [
            contract_rows(
                hidden_rim[offset * frame_len : offset * frame_len + tok_local], grad_features
            )
            for offset in range(3)
        ]
    )
    grad_hidden = jnp.zeros((tok_local, channels), jnp.float32)
    for offset in range(3):
        grad_hidden = grad_hidden + jnp.dot(
            grad_rim[(2 - offset) * frame_len : (2 - offset) * frame_len + tok_local],
            w_temporal[offset].T,
            preferred_element_type=jnp.float32,
        )
    grad_pre = (grad_hidden * silu_slope(pre_act)).astype(jnp.bfloat16)
    grad_ws = jnp.stack([contract_rows(taps[offset], grad_pre) for offset in range(9)])
    totals = lax.psum(
        (grad_ws, grad_wt, grad_wq_local, grad_wk_local, grad_wv_local, grad_wo_local),
        ("frame", "dp"),
    )
    factor = float(lax.axis_size("dp") * lax.axis_size("frame") * tok_local) ** (-0.5)
    return (
        totals[0] * factor,
        totals[1] * factor,
        totals[2] * factor,
        totals[3] * factor,
        totals[4] * factor,
        totals[5] * factor,
    )


def solution(mesh):
    in_specs = (
        P("dp", "frame", None),
        P("dp", None),
        P(),
        P(),
        P(None, "head"),
        P(None, "head"),
        P(None, "head"),
        P("head", None),
        P("dp", "frame", None),
    )
    out_specs = (P(), P(), P(None, "head"), P(None, "head"), P(None, "head"), P("head", None))
    return jax.shard_map(
        on_device, mesh=mesh, in_specs=in_specs, out_specs=out_specs, check_vma=False
    )
```

profile of v0, /device:TPU:8, one launch (start us, length us, event | category | flops | bytes accessed | tf_op | source)
XLA Modules:
  0.0 700.0 jit_solution(11616659482293236148)
XLA Ops:
  7.2 1.9 pad_slice_fusion
  9.2 1.2 fusion.60
  10.4 1.1 convolution_add_fusion.11
  13.6 4.0 collective-permute-start
  17.6 1.3 collective-permute-start.1
  19.1 4.3 collective-permute-done.1
  24.8 1.7 convolution_convert_fusion
  27.7 85.4 %all-gather.3.cloned.1.call-done = bf16[4096,256]{1,0:T(8,128)(2,1)} async-done(((bf16[256,256]{1,0:T(8,128)(2,1)}), bf16[4096,256]{1,0:T(8,128)(2,1)}) %all-gather.3.cloned.1.call-update) | async-done | bytes 2097168 | tf_op jit(solution)/shard_map/all_gather | solution.py:90
  113.1 2.3 fusion.108
  116.3 1.9 fusion.6
  118.7 2.4 fusion.9
  121.1 1.3 copy-done.1
  122.4 1.8 fusion.91
  124.2 1.8 fusion.94
  126.0 72.5 %all-gather.5.cloned.1.call-done = bf16[4096,256]{1,0:T(8,128)(2,1)} async-done(((bf16[256,256]{1,0:T(8,128)(2,1)}), bf16[4096,256]{1,0:T(8,128)(2,1)}) %all-gather.5.cloned.1.call-update) | async-done | bytes 2097168 | tf_op jit(solution)/shard_map/all_gather | solution.py:91
  198.4 2.8 convolution_convert_fusion.5
  201.3 2.9 multiply_reduce_fusion.1
  204.3 1.7 fusion.5
  206.5 1.7 copy-done.4
  208.1 1.7 fusion.4
  209.8 1.3 copy-done.2
  211.6 1.1 copy-done.7
  213.4 3.8 pad_maximum_fusion
  217.4 2.8 convolution_convert_fusion.6
  223.3 216.4 %reduce-scatter.2.cloned.1.call-done = f32[256,512]{0,1:T(8,128)} async-done(((f32[4096,512]{0,1:T(8,128)}), f32[256,512]{0,1:T(8,128)}) %reduce-scatter.2.cloned.1.call-update) | async-done | bytes 524304 | tf_op jit(solution)/shard_map/reduce_scatter | solution.py:147
  439.7 1.1 convert.4
  443.9 60.5 %all-reduce.5.cloned.1.call-done = f32[256,256]{1,0:T(8,128)} async-done(((f32[256,256]{1,0:T(8,128)}), f32[256,256]{1,0:T(8,128)}) %all-reduce.5.cloned.1.call-update) | async-done | bytes 262160 | tf_op jit(solution)/shard_map/psum | solution.py:159
  505.8 1.3 collective-permute-start.2
  507.1 4.5 collective-permute-start.3
  515.8 1.4 copy-done.9
  517.3 168.9 %all-reduce.7.cloned.1.call-done = (f32[9,256,256]{2,1,0:T(8,128)}, f32[3,256,256]{2,1,0:T(8,128)}, f32[256,256]{1,0:T(8,128)}, f32[256,256]{1,0:T(8,128)}, f32[256,256]{1,0:T(8,128)}, /*index=5*/f32[256,256]{1,0:T(8,128)}) async-done(((f32[9,256,256]{2,1,0:T(8,128)}, f32[3,256,256]{2,1,0:T(8,128)}, f32[256,256]{1,0:T(8,128)}, f32[256,256]{1,0:T(8,128)}, f32[256,256]{1,0:T(8,128)}, ...) | async-done | bytes 4194320 | tf_op jit(solution)/shard_map/psum | solution.py:179
  686.1 3.4 broadcast_multiply_fusion
  (158 shorter events, 23.3 us)
Async XLA Ops:
  7.2 20.4 %copy-start = (bf16[256,256]{1,0:T(8,128)(2,1)S(1)}, bf16[256,256]{1,0:T(8,128)(2,1)}, u32[]{:S(2)}) copy-start(bf16[256,256]{1,0:T(8,128)(2,1)} %param.13) | copy-start | bytes 393220
  7.2 4.7 copy-start.14
  7.2 4.3 copy-start.19
  7.2 105.9 %all-gather.3.cloned.1.call-start = ((), (), s32[]{:S(2)}) async-start(), calls=%async_computation.1 | async-start | bytes 2228224 | tf_op jit(solution)/shard_map/all_gather | solution.py:90
  11.9 7.0 %copy-start.17 = (bf16[3,256,256]{2,1,0:T(8,128)(2,1)S(1)}, bf16[3,256,256]{2,1,0:T(8,128)(2,1)}, u32[]{:S(2)}) copy-start(bf16[3,256,256]{2,1,0:T(8,128)(2,1)} %param.12) | copy-start | bytes 1179652
  12.5 11.3 %copy-start.27 = (bf16[256,256]{1,0:T(8,128)(2,1)S(1)}, bf16[256,256]{1,0:T(8,128)(2,1)}, u32[]{:S(2)}) copy-start(bf16[256,256]{1,0:T(8,128)(2,1)} %param.14) | copy-start | bytes 393220
  12.7 13.9 %copy-start.42 = (s32[1,4096]{1,0:T(1,128)S(1)}, s32[1,4096]{1,0:T(1,128)}, u32[]{:S(2)}) copy-start(s32[1,4096]{1,0:T(1,128)} %param.10) | copy-start | bytes 49156
  12.7 13.9 %copy-start.13 = (bf16[1,256,256]{2,1,0:T(8,128)(2,1)S(1)}, bf16[1,256,256]{2,1,0:T(8,128)(2,1)}, u32[]{:S(2)}) copy-start(bf16[1,256,256]{2,1,0:T(8,128)(2,1)} %param.17) | copy-start | bytes 393220
  13.6 13.0 %copy-start.37 = (bf16[256,256]{1,0:T(8,128)(2,1)S(1)}, bf16[256,256]{1,0:T(8,128)(2,1)}, u32[]{:S(2)}) copy-start(bf16[256,256]{1,0:T(8,128)(2,1)} %param.16) | copy-start | bytes 393220
  13.6 10.0 %collective-permute-start = (bf16[64,256]{1,0:T(8,128)(2,1)S(1)}, bf16[64,256]{1,0:T(8,128)(2,1)S(1)}, u32[]{:S(2)}, u32[]{:S(2)}) collective-permute-start(bf16[64,256]{1,0:T(8,128)(2,1)S(1)} %get-tuple-element.18), channel_id=1, source_target_pairs={{0,16},{16,32},{32,48},{48,64},{64,80},{80,96},{96,112},{112,128},... | collective-permute-start | bytes 98312 | tf_op jit(solution)/shard_map/ppermute | solution.py:19
  17.6 5.8 collective-permute-start.1
  23.4 91.9 %copy-start.38 = (bf16[64,256]{1,0:T(8,128)(2,1)}, bf16[64,256]{1,0:T(8,128)(2,1)S(1)}, u32[]{:S(2)}) copy-start(bf16[64,256]{1,0:T(8,128)(2,1)S(1)} %collective-permute-done.1) | copy-start | bytes 98308
  23.6 91.7 %copy-start.40 = (bf16[64,256]{1,0:T(8,128)(2,1)}, bf16[64,256]{1,0:T(8,128)(2,1)S(1)}, u32[]{:S(2)}) copy-start(bf16[64,256]{1,0:T(8,128)(2,1)S(1)} %collective-permute-done) | copy-start | bytes 98308
  24.7 173.7 %all-gather.5.cloned.1.call-start = ((), (), s32[]{:S(2)}) async-start(), calls=%async_computation.2 | async-start | bytes 2228224 | tf_op jit(solution)/shard_map/all_gather | solution.py:91
  26.5 413.2 %reduce-scatter.2.cloned.1.call-start = ((), (), s32[]{:S(2)}) async-start(), calls=%async_computation.3 | async-start | bytes 8912896 | tf_op jit(solution)/shard_map/reduce_scatter | solution.py:147
  26.6 89.7 %copy-start.43 = (s32[1,256]{1,0:T(1,128)}, s32[1,256]{1,0:T(1,128)S(1)}, u32[]{:S(2)}) copy-start(s32[1,256]{1,0:T(1,128)S(1)} %constant_dynamic-slice_fusion) | copy-start | bytes 3076
  27.7 87.6 %copy-start.25 = (bf16[256,256]{1,0:T(8,128)(2,1)}, bf16[256,256]{1,0:T(8,128)(2,1)S(1)}, u32[]{:S(2)}) copy-start(bf16[256,256]{1,0:T(8,128)(2,1)S(1)} %convolution_convert_fusion.3) | copy-start | bytes 393220
  198.4 5.8 copy-start.6
  201.3 4.7 copy-start.23
  217.2 287.1 %all-reduce.5.cloned.1.call-start = ((), (), s32[]{:S(2)}) async-start(), calls=%async_computation.4 | async-start | bytes 524288 | tf_op jit(solution)/shard_map/psum | solution.py:159
  221.2 220.5 %copy-start.28 = (bf16[256,256]{1,0:T(8,128)(2,1)S(1)}, bf16[256,256]{1,0:T(8,128)(2,1)}, u32[]{:S(2)}) copy-start(bf16[256,256]{1,0:T(8,128)(2,1)} %param.14) | copy-start | bytes 393220
  221.2 220.8 %copy-start.29 = (bf16[256,256]{1,0:T(8,128)(2,1)S(1)}, bf16[256,256]{1,0:T(8,128)(2,1)}, u32[]{:S(2)}) copy-start(bf16[256,256]{1,0:T(8,128)(2,1)} %param.15) | copy-start | bytes 393220
  223.3 282.3 %copy-start.18 = (bf16[3,256,256]{2,1,0:T(8,128)(2,1)S(1)}, bf16[3,256,256]{2,1,0:T(8,128)(2,1)}, u32[]{:S(2)}) copy-start(bf16[3,256,256]{2,1,0:T(8,128)(2,1)} %param.12) | copy-start | bytes 1179652
  440.8 70.9 %copy-start.41 = (bf16[64,256]{1,0:T(8,128)(2,1)S(1)}, bf16[64,256]{1,0:T(8,128)(2,1)}, u32[]{:S(2)}) copy-start(bf16[64,256]{1,0:T(8,128)(2,1)} %copy-done.40) | copy-start | bytes 98308
  441.7 70.2 %copy-start.39 = (bf16[64,256]{1,0:T(8,128)(2,1)S(1)}, bf16[64,256]{1,0:T(8,128)(2,1)}, u32[]{:S(2)}) copy-start(bf16[64,256]{1,0:T(8,128)(2,1)} %copy-done.38) | copy-start | bytes 98308
  442.9 243.2 %all-reduce.7.cloned.1.call-start = ((), (), s32[]{:S(2)}) async-start(), calls=%async_computation.5 | async-start | bytes 8388608 | tf_op jit(solution)/shard_map/psum | solution.py:179
  443.9 69.6 %copy-start.49 = (f32[256,256]{1,0:T(8,128)S(1)}, f32[256,256]{1,0:T(8,128)}, u32[]{:S(2)}) copy-start(f32[256,256]{1,0:T(8,128)} %get-tuple-element.31) | copy-start | bytes 786436
  505.8 7.7 %collective-permute-start.2 = (bf16[64,256]{1,0:T(8,128)(2,1)S(1)}, bf16[64,256]{1,0:T(8,128)(2,1)S(1)}, u32[]{:S(2)}, u32[]{:S(2)}) collective-permute-start(bf16[64,256]{1,0:T(8,128)(2,1)S(1)} %get-tuple-element.16), channel_id=1, source_target_pairs={{16,0},{32,16},{48,32},{64,48},{80,64},{96,80},{112,96},{128,112},... | collective-permute-start | bytes 98312 | tf_op jit(solution)/shard_map/ppermute | solution.py:21
  507.1 6.1 collective-permute-start.3
  686.1 4.9 copy-start.33
  686.1 5.6 copy-start.32
  686.1 6.3 copy-start.22
  (27 other events, 67.7 us)
Sparse Core Ops, SparseCore 0:
  24.8 88.2 all-gather.2
  116.2 82.1 all-gather.4
  217.3 222.3 reduce-scatter.1
  443.1 61.2 all-reduce.4
  517.4 168.7 all-reduce.6
where the time goes:
time: 700 us
  waiting for transfers between devices  608 us (87%)
  matrix products  37.3 us (5%)
  other arithmetic  18.4 us (3%)
  between operations  14.7 us (2%)
  starting transfers between devices  11.5 us (2%)
  local copies, waits for them, and re-layouts  9.96 us (1%)
    reduce_scatter x1, waiting for transfers between devices, on_device(): lax.psum_scatter(jnp.concatenate(key_parts + value_parts, axis=1), 'frame...  216 us
    psum x1, waiting for transfers between devices, on_device(): lax.psum((grad_ws, grad_wt, grad_wq_local, grad_wk_local, grad_wv_local,...  169 us
    all_gather x1, waiting for transfers between devices, on_device(): lax.all_gather(keys_local, 'frame', axis=0, tiled=True)  85.4 us
    all_gather x1, waiting for transfers between devices, on_device(): lax.all_gather(values_local, 'frame', axis=0, tiled=True)  72.5 us
    psum x1, waiting for transfers between devices, on_device(): head_sum = lax.psum(back_part, 'head')  60.5 us
  transfers between devices with their start and end apart: 9, of which 7 were waited for; matrix products, arithmetic and copies ran while one was open for 3% of the time, Pallas kernels for 0%

commit v1 on v0

--- a/solution.py
+++ b/solution.py
@@ -88,7 +88,10 @@
     )
     keys_every, values_every = (
         lax.all_gather(keys_local, "frame", axis=0, tiled=True),
-        lax.all_gather(values_local, "frame", axis=0, tiled=True),
+        jnp.concatenate(
+            lax.all_to_all(jnp.stack([values_local] * lax.axis_size("frame")), "frame", 0, 0),
+            axis=0,
+        ),
     )
     first_row = lax.axis_index("frame") * tok_local
     grad_attended = jnp.dot(upstream, w_out.T, preferred_element_type=jnp.float32).astype(

time: 700 us -> 639 us (0.913)
  waiting for transfers between devices: 608 us -> 540 us
  starting transfers between devices: 11.5 us -> 22.2 us
    all_gather x1 -> x0, waiting for transfers between devices: 72.5 us -> none  [on_device(): lax.all_gather(values_local, 'frame', axis=0, tiled=True)]
    all_to_all x0 -> x1, starting transfers between devices: none -> 11.1 us  [on_device(): lax.all_to_all(jnp.stack([values_local] * lax.axis_size('frame')), 'frame...]
  transfers between devices with their start and end apart: 9 -> 9, of which waited for: 7 -> 6; matrix products, arithmetic and copies ran while one was open for 3% -> 3% of each run, Pallas kernels for 0% -> 0%
where the time goes in v1:
time: 639 us
  waiting for transfers between devices  540 us (85%)
  matrix products  35.8 us (6%)
  starting transfers between devices  22.2 us (3%)
  other arithmetic  19.4 us (3%)
  between operations  14.6 us (2%)
  local copies, waits for them, and re-layouts  6.8 us (1%)
    reduce_scatter x1, waiting for transfers between devices, on_device(): lax.psum_scatter(jnp.concatenate(key_parts + value_parts, axis=1), 'frame...  217 us
    psum x1, waiting for transfers between devices, on_device(): lax.psum((grad_ws, grad_wt, grad_wq_local, grad_wk_local, grad_wv_local,...  169 us
    all_gather x1, waiting for transfers between devices, on_device(): lax.all_gather(keys_local, 'frame', axis=0, tiled=True)  89.5 us
    psum x1, waiting for transfers between devices, on_device(): head_sum = lax.psum(back_part, 'head')  60.3 us
  transfers between devices with their start and end apart: 9, of which 6 were waited for; matrix products, arithmetic and copies ran while one was open for 3% of the time, Pallas kernels for 0%

profile of v1, /device:TPU:8, one launch (start us, length us, event | category | flops | bytes accessed | tf_op | source)
XLA Modules:
  0.0 639.0 jit_solution(5434377216177554321)
XLA Ops:
  7.2 1.9 pad_slice_fusion
  9.2 1.2 fusion.60
  10.4 1.1 convolution_add_fusion.11
  13.6 3.8 collective-permute-start
  17.4 1.3 collective-permute-start.1
  18.9 4.3 collective-permute-done.1
  25.2 1.5 stack.30
  26.7 11.1 %all-to-all-start = ((bf16[16,256,256]{2,1,0:T(8,128)(2,1)}), bf16[16,256,256]{2,1,0:T(8,128)(2,1)}, u32[]{:S(2)}, u32[]{:S(2)}) async-start(bf16[16,256,256]{2,1,0:T(8,128)(2,1)} %stack.30), calls=%async_computation | async-start | bytes 4194304 | tf_op jit(solution)/shard_map/all_to_all | solution.py:92
  39.0 89.5 %all-gather.2.cloned.1.call-done = bf16[4096,256]{1,0:T(8,128)(2,1)} async-done(((bf16[256,256]{1,0:T(8,128)(2,1)}), bf16[4096,256]{1,0:T(8,128)(2,1)}) %all-gather.2.cloned.1.call-update) | async-done | bytes 2097168 | tf_op jit(solution)/shard_map/all_gather | solution.py:90
  128.5 2.3 fusion.108
  131.7 1.9 fusion.6
  134.2 3.4 fusion.9
  137.6 2.8 convolution_convert_fusion.5
  141.4 3.0 multiply_reduce_fusion.1
  144.4 3.0 fusion.5
  147.5 2.9 fusion.4
  152.2 3.8 pad_maximum_fusion
  156.2 2.8 convolution_convert_fusion.6
  159.9 0.9 fusion.83
  162.0 216.9 %reduce-scatter.2.cloned.1.call-done = f32[256,512]{0,1:T(8,128)} async-done(((f32[4096,512]{0,1:T(8,128)}), f32[256,512]{0,1:T(8,128)}) %reduce-scatter.2.cloned.1.call-update) | async-done | bytes 524304 | tf_op jit(solution)/shard_map/reduce_scatter | solution.py:150
  378.9 1.1 convert.4
  381.2 0.9 convolution_add_fusion.1
  382.2 0.9 fusion.71
  383.1 60.3 %all-reduce.5.cloned.1.call-done = f32[256,256]{1,0:T(8,128)} async-done(((f32[256,256]{1,0:T(8,128)}), f32[256,256]{1,0:T(8,128)}) %all-reduce.5.cloned.1.call-update) | async-done | bytes 262160 | tf_op jit(solution)/shard_map/psum | solution.py:162
  443.4 1.0 add_convert_fusion
  444.9 1.3 collective-permute-start.2
  446.2 4.5 collective-permute-start.3
  451.2 0.9 pad_maximum_fusion.1
  454.9 1.4 copy-done.7
  456.3 168.8 %all-reduce.7.cloned.1.call-done = (f32[9,256,256]{2,1,0:T(8,128)}, f32[3,256,256]{2,1,0:T(8,128)}, f32[256,256]{1,0:T(8,128)}, f32[256,256]{1,0:T(8,128)}, f32[256,256]{1,0:T(8,128)}, /*index=5*/f32[256,256]{1,0:T(8,128)}) async-done(((f32[9,256,256]{2,1,0:T(8,128)}, f32[3,256,256]{2,1,0:T(8,128)}, f32[256,256]{1,0:T(8,128)}, f32[256,256]{1,0:T(8,128)}, f32[256,256]{1,0:T(8,128)}, ...) | async-done | bytes 4194320 | tf_op jit(solution)/shard_map/psum | solution.py:182
  625.1 3.4 broadcast_multiply_fusion
  631.5 0.9 broadcast_multiply_fusion.1
  (152 shorter events, 19.2 us)
Async XLA Ops:
  7.2 31.6 %copy-start = (bf16[256,256]{1,0:T(8,128)(2,1)S(1)}, bf16[256,256]{1,0:T(8,128)(2,1)}, u32[]{:S(2)}) copy-start(bf16[256,256]{1,0:T(8,128)(2,1)} %param.13) | copy-start | bytes 393220
  7.2 4.7 copy-start.11
  7.2 4.3 copy-start.16
  7.2 121.3 %all-gather.2.cloned.1.call-start = ((), (), s32[]{:S(2)}) async-start(), calls=%async_computation.2 | async-start | bytes 2228224 | tf_op jit(solution)/shard_map/all_gather | solution.py:90
  9.2 3.5 copy-start.27
  11.9 6.9 %copy-start.14 = (bf16[3,256,256]{2,1,0:T(8,128)(2,1)S(1)}, bf16[3,256,256]{2,1,0:T(8,128)(2,1)}, u32[]{:S(2)}) copy-start(bf16[3,256,256]{2,1,0:T(8,128)(2,1)} %param.12) | copy-start | bytes 1179652
  12.5 11.6 %copy-start.23 = (bf16[256,256]{1,0:T(8,128)(2,1)S(1)}, bf16[256,256]{1,0:T(8,128)(2,1)}, u32[]{:S(2)}) copy-start(bf16[256,256]{1,0:T(8,128)(2,1)} %param.14) | copy-start | bytes 393220
  12.5 12.4 %copy-start.25 = (bf16[256,256]{1,0:T(8,128)(2,1)S(1)}, bf16[256,256]{1,0:T(8,128)(2,1)}, u32[]{:S(2)}) copy-start(bf16[256,256]{1,0:T(8,128)(2,1)} %param.15) | copy-start | bytes 393220
  13.6 10.2 %collective-permute-start = (bf16[64,256]{1,0:T(8,128)(2,1)S(1)}, bf16[64,256]{1,0:T(8,128)(2,1)S(1)}, u32[]{:S(2)}, u32[]{:S(2)}) collective-permute-start(bf16[64,256]{1,0:T(8,128)(2,1)S(1)} %get-tuple-element.18), channel_id=1, source_target_pairs={{0,16},{16,32},{32,48},{48,64},{64,80},{80,96},{96,112},{112,128},... | collective-permute-start | bytes 98312 | tf_op jit(solution)/shard_map/ppermute | solution.py:19
  17.4 5.8 collective-permute-start.1
  26.7 11.2 %copy-start.39 = (s32[1,4096]{1,0:T(1,128)S(1)}, s32[1,4096]{1,0:T(1,128)}, u32[]{:S(2)}) copy-start(s32[1,4096]{1,0:T(1,128)} %param.10) | copy-start | bytes 49156
  26.7 11.2 %copy-start.10 = (bf16[1,256,256]{2,1,0:T(8,128)(2,1)S(1)}, bf16[1,256,256]{2,1,0:T(8,128)(2,1)}, u32[]{:S(2)}) copy-start(bf16[1,256,256]{2,1,0:T(8,128)(2,1)} %param.17) | copy-start | bytes 393220
  26.7 11.2 %copy-start.34 = (bf16[256,256]{1,0:T(8,128)(2,1)S(1)}, bf16[256,256]{1,0:T(8,128)(2,1)}, u32[]{:S(2)}) copy-start(bf16[256,256]{1,0:T(8,128)(2,1)} %param.16) | copy-start | bytes 393220
  26.7 110.9 %all-to-all-start = ((bf16[16,256,256]{2,1,0:T(8,128)(2,1)}), bf16[16,256,256]{2,1,0:T(8,128)(2,1)}, u32[]{:S(2)}, u32[]{:S(2)}) async-start(bf16[16,256,256]{2,1,0:T(8,128)(2,1)} %stack.30), calls=%async_computation | async-start | bytes 4194304 | tf_op jit(solution)/shard_map/all_to_all | solution.py:92
  37.8 341.1 %reduce-scatter.2.cloned.1.call-start = ((), (), s32[]{:S(2)}) async-start(), calls=%async_computation.3 | async-start | bytes 8912896 | tf_op jit(solution)/shard_map/reduce_scatter | solution.py:150
  37.9 93.8 %copy-start.40 = (s32[1,256]{1,0:T(1,128)}, s32[1,256]{1,0:T(1,128)S(1)}, u32[]{:S(2)}) copy-start(s32[1,256]{1,0:T(1,128)S(1)} %constant_dynamic-slice_fusion) | copy-start | bytes 3076
  39.0 91.8 %copy-start.21 = (bf16[256,256]{1,0:T(8,128)(2,1)}, bf16[256,256]{1,0:T(8,128)(2,1)S(1)}, u32[]{:S(2)}) copy-start(bf16[256,256]{1,0:T(8,128)(2,1)S(1)} %convolution_convert_fusion.3) | copy-start | bytes 393220
  140.9 3.5 copy-start.6
  156.1 287.3 %all-reduce.5.cloned.1.call-start = ((), (), s32[]{:S(2)}) async-start(), calls=%async_computation.4 | async-start | bytes 524288 | tf_op jit(solution)/shard_map/psum | solution.py:162
  159.9 221.0 %copy-start.24 = (bf16[256,256]{1,0:T(8,128)(2,1)S(1)}, bf16[256,256]{1,0:T(8,128)(2,1)}, u32[]{:S(2)}) copy-start(bf16[256,256]{1,0:T(8,128)(2,1)} %param.14) | copy-start | bytes 393220
  159.9 221.3 %copy-start.26 = (bf16[256,256]{1,0:T(8,128)(2,1)S(1)}, bf16[256,256]{1,0:T(8,128)(2,1)}, u32[]{:S(2)}) copy-start(bf16[256,256]{1,0:T(8,128)(2,1)} %param.15) | copy-start | bytes 393220
  162.0 282.6 %copy-start.15 = (bf16[3,256,256]{2,1,0:T(8,128)(2,1)S(1)}, bf16[3,256,256]{2,1,0:T(8,128)(2,1)}, u32[]{:S(2)}) copy-start(bf16[3,256,256]{2,1,0:T(8,128)(2,1)} %param.12) | copy-start | bytes 1179652
  380.0 70.7 %copy-start.38 = (bf16[64,256]{1,0:T(8,128)(2,1)S(1)}, bf16[64,256]{1,0:T(8,128)(2,1)}, u32[]{:S(2)}) copy-start(bf16[64,256]{1,0:T(8,128)(2,1)} %copy-done.37) | copy-start | bytes 98308
  380.9 70.0 %copy-start.36 = (bf16[64,256]{1,0:T(8,128)(2,1)S(1)}, bf16[64,256]{1,0:T(8,128)(2,1)}, u32[]{:S(2)}) copy-start(bf16[64,256]{1,0:T(8,128)(2,1)} %copy-done.35) | copy-start | bytes 98308
  382.1 243.0 %all-reduce.7.cloned.1.call-start = ((), (), s32[]{:S(2)}) async-start(), calls=%async_computation.5 | async-start | bytes 8388608 | tf_op jit(solution)/shard_map/psum | solution.py:182
  383.1 69.4 %copy-start.46 = (f32[256,256]{1,0:T(8,128)S(1)}, f32[256,256]{1,0:T(8,128)}, u32[]{:S(2)}) copy-start(f32[256,256]{1,0:T(8,128)} %get-tuple-element.31) | copy-start | bytes 786436
  444.9 7.7 %collective-permute-start.2 = (bf16[64,256]{1,0:T(8,128)(2,1)S(1)}, bf16[64,256]{1,0:T(8,128)(2,1)S(1)}, u32[]{:S(2)}, u32[]{:S(2)}) collective-permute-start(bf16[64,256]{1,0:T(8,128)(2,1)S(1)} %get-tuple-element.16), channel_id=1, source_target_pairs={{16,0},{32,16},{48,32},{64,48},{80,64},{96,80},{112,96},{128,112},... | collective-permute-start | bytes 98312 | tf_op jit(solution)/shard_map/ppermute | solution.py:21
  446.2 6.1 collective-permute-start.3
  625.1 4.2 copy-start.31
  625.1 4.9 copy-start.30
  625.1 5.6 copy-start.29
  625.1 6.3 copy-start.18
  (24 other events, 52.4 us)
Sparse Core Ops, SparseCore 0:
  25.1 103.3 all-gather.1
  156.2 222.6 reduce-scatter.1
  382.2 61.1 all-reduce.4
  456.4 168.6 all-reduce.6
